TPU v7x, 128 devices: a whole 4x4x4 slice. The times are simulated.
128 devices in a mesh: group: 2 (over x_hi), dev: 64 (over z, x_lo, y, core).
Axes of the slice: x: 4 (x_hi: 2, x_lo: 2; x = x_hi * 2 + x_lo), y: 4, z: 4, core: 2. Of those that a mesh axis runs over, the one named last changes fastest.
Arguments:
- query_latent: bfloat16 [512, 128, 512], P(('group', 'dev')), may hold values from -100 to 100
- query_rope: bfloat16 [512, 128, 64], P(('group', 'dev')), may hold values from -3 to 3
- cache_latent: bfloat16 [512, 2048, 512], P(('group', 'dev')), may hold values from -6 to 6
- cache_rope: bfloat16 [512, 64, 2048], P(('group', 'dev')), may hold values from -6 to 6
- lengths: int32 [512], P(('group', 'dev')), may hold values from 256 to 2048
- value_up: bfloat16 [128, 512, 128], P('dev'), may hold values from -0.25 to 0.25
- out_proj: bfloat16 [16384, 7168], P('dev'), may hold values from -0.046875 to 0.046875
- residual: bfloat16 [512, 7168], P(('group', 'dev')), may hold values from -6 to 6
- norm_gain: float32 [7168], replicated, may hold values from 0.25 to 1.75
- expert_ids: int32 [512, 8], P(('group', 'dev')), may hold values from 0 to 31, all different within a row; in each aligned block of 4 rows (0 to 3, 4 to 7, ...) at most 2 rows name the same one
- gate_values: float32 [512, 8], P(('group', 'dev')), may hold values from 0.1 to 1
- w_gate: bfloat16 [64, 7168, 512], P('dev', None, 'group'), may hold values from -0.0625 to 0.0625
- w_up: bfloat16 [64, 7168, 512], P('dev', None, 'group'), may hold values from -0.0625 to 0.0625
- w_down: bfloat16 [64, 512, 7168], P('dev', 'group'), may hold values from -0.1875 to 0.1875
Outputs:
- layer_out: bfloat16 [512, 7168], P(('group', 'dev'))
Inputs may be any that keep to these rules, and one draw needn't show every extreme that they name: `expert_ids`: each row names 8 different experts. Among the rows of one device no expert is named by more than 2 rows, and in every draw some expert is named by exactly 2 rows of some device.
All inputs are finite; a program needn't handle non-finite values.
Results may differ from a plain program's by a relative error of at most 0.008.
Values may be sent and summed in bfloat16 or wider, within the bound.
A program may use at most 128 MiB of HBM per device.

v0:
```python
import jax
import jax.numpy as jnp
from jax import lax
from jax.sharding import Mesh
from jax.sharding import PartitionSpec as P

DEV = ("dev_0", "dev_1", "dev_2", "dev_3")
GROUP_DEV = ("group", "dev_0", "dev_1", "dev_2", "dev_3")
softmax_scale = 192.0 ** (-0.5)


def attend(query_latent, query_rope, cache_latent, cache_rope, lengths):
    scores = jnp.einsum(
        "thl,tcl->thc", query_latent, cache_latent, preferred_element_type=jnp.float32
    )
    scores = scores + jnp.einsum(
        "thr,trc->thc", query_rope, cache_rope, preferred_element_type=jnp.float32
    )
    scores = scores * softmax_scale
    positions = lax.broadcasted_iota(jnp.int32, scores.shape, 2)
    scores = jnp.where(positions < lengths[:, None, None], scores, -jnp.inf)
    row_peak = jnp.max(scores, axis=2, keepdims=True)
    weights = jnp.exp(scores - row_peak)
    attn_weights = (weights / jnp.sum(weights, axis=2, keepdims=True)).astype(jnp.bfloat16)
    return jnp.einsum(
        "thc,tcl->thl", attn_weights, cache_latent, preferred_element_type=jnp.float32
    ).astype(jnp.bfloat16)


def expert_rows(token_rows, w_gate, w_up, w_down):
    gate_part = jnp.dot(token_rows, w_gate[0], preferred_element_type=jnp.float32)
    up_part = jnp.dot(token_rows, w_up[0], preferred_element_type=jnp.float32)
    active = (jax.nn.silu(gate_part) * up_part).astype(jnp.bfloat16)
    return jnp.dot(active, w_down[0], preferred_element_type=jnp.float32)


def local(
    query_latent,
    query_rope,
    cache_latent,
    cache_rope,
    lengths,
    value_up,
    out_proj,
    residual,
    norm_gain,
    expert_ids,
    gate_values,
    w_gate,
    w_up,
    w_down,
):
    tok_rows = query_latent.shape[0]
    feature_width = residual.shape[1]
    mixed_latent = attend(query_latent, query_rope, cache_latent, cache_rope, lengths)
    by_head = lax.all_to_all(mixed_latent, DEV, split_axis=1, concat_axis=0, tiled=True)
    head_values = jnp.einsum(
        "thl,hlv->thv", by_head, value_up, preferred_element_type=jnp.float32
    ).astype(jnp.bfloat16)
    flat_values = head_values.reshape(head_values.shape[0], -1)
    attention_part = jnp.dot(flat_values, out_proj, preferred_element_type=jnp.float32)
    attention = lax.psum_scatter(
        attention_part.astype(jnp.bfloat16), DEV, scatter_dimension=0, tiled=True
    ).astype(jnp.float32)
    stream = residual.astype(jnp.float32) + attention
    normed = (
        stream * lax.rsqrt(jnp.mean(stream * stream, axis=1, keepdims=True) + 1e-06) * norm_gain
    ).astype(jnp.bfloat16)
    experts = lax.axis_size(DEV) // 2
    expert_range = jnp.arange(experts, dtype=jnp.int32)
    chosen = expert_ids[:, :, None] == expert_range[None, None, :]
    row_gates = jnp.sum(jnp.where(chosen, gate_values[:, :, None], 0.0), axis=1)
    all_rows = lax.all_gather(normed, GROUP_DEV, axis=0, tiled=True)
    all_gates = lax.all_gather(row_gates, GROUP_DEV, axis=0, tiled=True)
    mine = lax.axis_index(DEV) // 2
    my_gates = jnp.sum(jnp.where(expert_range[None, :] == mine, all_gates, 0.0), axis=1)
    partial_value = expert_rows(all_rows, w_gate, w_up, w_down) * my_gates[:, None]
    mixture = lax.psum_scatter(
        partial_value.astype(jnp.bfloat16), GROUP_DEV, scatter_dimension=0, tiled=True
    ).astype(jnp.float32)
    return (stream + mixture).astype(jnp.bfloat16)


def solution(mesh):
    finer = Mesh(
        mesh.devices.reshape(mesh.shape["group"], 4, 2, 4, 2),
        ("group", "dev_0", "dev_1", "dev_2", "dev_3"),
    )
    return jax.shard_map(
        local,
        mesh=finer,
        in_specs=(
            P(GROUP_DEV, None, None),
            P(GROUP_DEV, None, None),
            P(GROUP_DEV, None, None),
            P(GROUP_DEV, None, None),
            P(GROUP_DEV),
            P(DEV, None, None),
            P(DEV, None),
            P(GROUP_DEV, None),
            P(),
            P(GROUP_DEV, None),
            P(GROUP_DEV, None),
            P(DEV, None, "group"),
            P(DEV, None, "group"),
            P(DEV, "group", None),
        ),
        out_specs=P(GROUP_DEV, None),
        check_vma=False,
    )
```

profile of v0, /device:TPU:1, one launch (start us, length us, event | category | flops | bytes accessed | tf_op | source)
XLA Modules:
  0.0 1019.2 jit_solution(3751967246180345959)
XLA Ops:
  6.5 0.0 copy-start
  6.5 0.0 copy-start.9
  6.5 0.0 copy-start.3
  6.5 0.0 all-reduce.5.cloned.1.call-start
  6.5 1.2 copy-done
  7.8 1.6 fusion.22
  9.3 0.0 copy-done.9
  9.4 0.0 copy-done.3
  9.4 6.3 multiply_select_fusion
  15.7 0.0 copy-start.2
  15.7 1.9 copy-done.2
  17.6 0.8 fusion.21
  18.4 7.6 fusion.8
  26.0 0.0 copy-start.5
  26.0 0.4 copy.20
  26.4 23.2 %all_to_all.18 = bf16[4,128,512]{2,0,1:T(4,128)(2,1)S(1)} all-to-all(bf16[4,128,512]{2,0,1:T(4,128)(2,1)S(1)} %copy.20), channel_id=1, replica_groups=mesh['group'=2,'dev_0'=4,'dev_1'=2,'dev_2'=4,'dev_3'=2] {'dev_0','dev_1'..., dimensions={1} | all-to-all | bytes 1048576 | tf_op jit(solution)/shard_map/all_to_all | solution.py:56
  49.6 0.2 copy.25
  49.8 0.1 all_to_all.16
  49.9 0.0 copy-done.5
  49.9 0.3 convolution_convert_fusion.1
  50.3 0.0 copy-start.10
  50.3 0.0 copy-start.4
  50.3 0.0 copy-start.6
  50.3 0.0 copy-start.7
  50.3 0.0 copy-start.8
  50.3 5.0 convolution_convert_fusion
  55.3 0.0 all-reduce.5.cloned.1.call-update
  55.4 0.0 all-gather.4.cloned.1.call-start
  55.4 0.0 copy-done.10
  55.4 0.6 dynamic-slice
  56.7 557.5 %all-reduce.5.cloned.1.call-done = bf16[256,7168]{1,0:T(8,128)(2,1)} async-done(((bf16[256,7168]{1,0:T(8,128)(2,1)}), bf16[256,7168]{1,0:T(8,128)(2,1)}) %all-reduce.5.cloned.1.call-update) | async-done | bytes 3670032
  614.1 0.0 copy-done.4
  614.1 1.1 multiply_reduce_fusion
  615.2 0.0 copy-done.6
  615.2 1.6 fusion.18
  616.8 0.0 all-gather.4.cloned.1.call-update
  616.9 0.0 all-reduce.7.cloned.1.call-start
  616.9 0.0 copy-done.7
  616.9 0.0 copy-done.8
  616.9 0.1 select_reduce_fusion.1
  617.0 177.6 %all-gather.1 = f32[128,4,32]{2,1,0:T(4,128)S(1)} all-gather(f32[1,4,32]{2,1,0:T(4,128)S(1)} %bitcast.46), channel_id=1, replica_groups=mesh['group'=2,'dev_0'=4,'dev_1'=2,'dev_2'=4,'dev_3'=2] {'group','dev_0'..., dimensions={0}, use_global_device_ids=true | all-gather | bytes 66048 | tf_op jit(solution)/shard_map/all_gather | solution.py:74
  794.6 0.1 select_reduce_fusion
  794.8 23.3 %all-gather.4.cloned.1.call-done = bf16[128,4,7168]{2,1,0:T(4,128)(2,1)} async-done(((bf16[1,4,7168]{2,1,0:T(4,128)(2,1)}), bf16[128,4,7168]{2,1,0:T(4,128)(2,1)}) %all-gather.4.cloned.1.call-update) | async-done | bytes 7340048 | tf_op jit(solution)/shard_map/all_gather | solution.py:73
  818.1 12.1 %reshape.25 = bf16[512,7168]{1,0:T(8,128)(2,1)} reshape(bf16[128,4,7168]{2,1,0:T(4,128)(2,1)} %all-gather.4.cloned.1.call-done) | data formatting | bytes 14680064
  830.2 6.2 fusion.4
  836.4 0.0 copy-start.1
  836.4 16.1 %multiply_convert_fusion = bf16[512,7168]{1,0:T(8,128)(2,1)} fusion(f32[512]{0:T(512)S(1)} %select_reduce_fusion, bf16[1,256,7168]{2,1,0:T(8,128)(2,1)} %param.27, bf16[512,7168]{1,0:T(8,128)(2,1)} %reshape.25, bf16[1,7168,256]{2,1,0:T(8,128)(2,1)} %param.26, f32[512,256]{1,0:T(8,128)S(1)} %fusion.4), kind=kOutput, calls=%fused_computation.1 | convolution fusion | flops 3766222848 | bytes 22546432 | tf_op jit(solution)/shard_map/dot_general | solution.py:34
  852.5 0.0 all-reduce.7.cloned.1.call-update
  852.5 158.5 %all-reduce.7.cloned.1.call-done = bf16[512,7168]{1,0:T(8,128)(2,1)} async-done(((bf16[512,7168]{1,0:T(8,128)(2,1)}), bf16[512,7168]{1,0:T(8,128)(2,1)}) %all-reduce.7.cloned.1.call-update) | async-done | bytes 7340048
  1011.1 1.7 add_convert_fusion
  1012.7 0.0 copy-done.1
  (2 shorter events, 0.0 us)
Async XLA Ops:
  6.5 1.2 copy-start
  6.5 2.8 copy-start.9
  6.5 2.8 copy-start.3
  6.5 607.6 %all-reduce.5.cloned.1.call-start = ((), (), s32[]{:S(2)}) async-start(), calls=%async_computation.2 | async-start | bytes 7340032
  15.7 1.9 copy-start.2
  26.0 23.9 %copy-start.5 = (bf16[2,512,128]{2,1,0:T(8,128)(2,1)S(1)}, bf16[2,512,128]{2,1,0:T(8,128)(2,1)}, u32[]{:S(2)}) copy-start(bf16[2,512,128]{2,1,0:T(8,128)(2,1)} %param.19) | copy-start | bytes 786436
  50.3 5.2 copy-start.10
  50.3 563.8 %copy-start.4 = (bf16[4,7168]{1,0:T(4,128)(2,1)S(1)}, bf16[4,7168]{1,0:T(4,128)(2,1)}, u32[]{:S(2)}) copy-start(bf16[4,7168]{1,0:T(4,128)(2,1)} %param.21) | copy-start | bytes 172036
  50.3 564.9 %copy-start.6 = (f32[7168]{0:T(1024)S(1)}, f32[7168]{0:T(1024)}, u32[]{:S(2)}) copy-start(f32[7168]{0:T(1024)} %param.22) | copy-start | bytes 86020
  50.3 566.6 %copy-start.7 = (f32[4,8]{1,0:T(4,128)S(1)}, f32[4,8]{1,0:T(4,128)}, u32[]{:S(2)}) copy-start(f32[4,8]{1,0:T(4,128)} %param.24) | copy-start | bytes 388
  50.3 566.6 %copy-start.8 = (s32[4,8]{1,0:T(4,128)S(1)}, s32[4,8]{1,0:T(4,128)}, u32[]{:S(2)}) copy-start(s32[4,8]{1,0:T(4,128)} %param.23) | copy-start | bytes 388
  55.4 762.8 %all-gather.4.cloned.1.call-start = ((), (), s32[]{:S(2)}) async-start(), calls=%async_computation.1 | async-start | bytes 7397376 | tf_op jit(solution)/shard_map/all_gather | solution.py:73
  616.9 394.2 %all-reduce.7.cloned.1.call-start = ((), (), s32[]{:S(2)}) async-start(), calls=%async_computation.3 | async-start | bytes 14680064
  836.4 176.3 %copy-start.1 = (bf16[4,64,2048]{2,1,0:T(8,128)(2,1)S(1)}, bf16[4,64,2048]{2,1,0:T(8,128)(2,1)}, u32[]{:S(2)}) copy-start(bf16[4,64,2048]{2,1,0:T(8,128)(2,1)} %param.17) | copy-start | bytes 3145732
Sparse Core Ops, SparseCore 0:
  55.5 558.5 all-reduce.4
  617.0 201.1 all-gather.3
  852.7 158.3 all-reduce.6
where the time goes:
time: 1020 us
  waiting for transfers between devices  739 us (72%)
  blocking collectives  201 us (20%)
  matrix products  43.1 us (4%)
  local copies, waits for them, and re-layouts  16.6 us (2%)
  between operations  14 us (1%)
    unnamed x5, waiting for transfers between devices  716 us
    all_gather x1, blocking collectives, local(): all_gates = lax.all_gather(row_gates, GROUP_DEV, axis=0, tiled=True)  178 us
    all_gather x1, waiting for transfers between devices, local(): all_rows = lax.all_gather(normed, GROUP_DEV, axis=0, tiled=True)  23.3 us
    all_to_all x1, blocking collectives, local(): lax.all_to_all(mixed_latent, DEV, split_axis=1, concat_axis=0, tiled=True)  23.2 us
  transfers between devices with their start and end apart: 3, of which 3 were waited for; matrix products, arithmetic and copies ran while one was open for 0% of the time, Pallas kernels for 0%

commit v1 on v0

--- a/solution.py
+++ b/solution.py
@@ -70,8 +70,11 @@
     expert_range = jnp.arange(experts, dtype=jnp.int32)
     chosen = expert_ids[:, :, None] == expert_range[None, None, :]
     row_gates = jnp.sum(jnp.where(chosen, gate_values[:, :, None], 0.0), axis=1)
-    all_rows = lax.all_gather(normed, GROUP_DEV, axis=0, tiled=True)
-    all_gates = lax.all_gather(row_gates, GROUP_DEV, axis=0, tiled=True)
+    all_rows, all_gates = jnp.split(
+        lax.all_gather(jnp.concatenate([normed, row_gates], axis=1), GROUP_DEV, axis=0, tiled=True),
+        [normed.shape[1]],
+        axis=1,
+    )
     mine = lax.axis_index(DEV) // 2
     my_gates = jnp.sum(jnp.where(expert_range[None, :] == mine, all_gates, 0.0), axis=1)
     partial_value = expert_rows(all_rows, w_gate, w_up, w_down) * my_gates[:, None]

time: 1020 us -> 1040 us (1.020)
  waiting for transfers between devices: 739 us -> 926 us
  blocking collectives: 201 us -> 23.2 us
    all_gather x1, waiting for transfers between devices: 23.3 us -> 210 us  [local(): lax.all_gather(jnp.concatenate([normed, row_gates], axis=1), GROUP_DEV, a...]
    all_gather x1 -> x0, blocking collectives: 178 us -> none  [local(): all_gates = lax.all_gather(row_gates, GROUP_DEV, axis=0, tiled=True)]
where the time goes in v1:
time: 1040 us
  waiting for transfers between devices  926 us (89%)
  matrix products  47.2 us (5%)
  blocking collectives  23.2 us (2%)
  local copies, waits for them, and re-layouts  22 us (2%)
  between operations  14 us (1%)
    unnamed x5, waiting for transfers between devices  716 us
    all_gather x1, waiting for transfers between devices, local(): lax.all_gather(jnp.concatenate([normed, row_gates], axis=1), GROUP_DEV, a...  210 us
    all_to_all x1, blocking collectives, local(): lax.all_to_all(mixed_latent, DEV, split_axis=1, concat_axis=0, tiled=True)  23.2 us
    unnamed x24, local copies, waits for them, and re-layouts  21.3 us
  transfers between devices with their start and end apart: 3, of which 3 were waited for; matrix products, arithmetic and copies ran while one was open for 0% of the time, Pallas kernels for 0%

profile of v1, /device:TPU:1, one launch (start us, length us, event | category | flops | bytes accessed | tf_op | source)
XLA Modules:
  0.0 1039.3 jit_solution(1325345807390456826)
XLA Ops:
  6.5 0.0 copy-start
  6.5 0.0 copy-start.3
  6.5 0.0 copy-start.9
  6.5 0.0 all-reduce.5.cloned.1.call-start
  6.5 1.2 copy-done
  7.8 1.6 fusion.30
  9.3 0.0 copy-done.3
  9.4 0.0 copy-done.9
  9.4 6.3 multiply_select_fusion
  15.7 0.0 copy-start.2
  15.7 1.9 copy-done.2
  17.6 0.8 fusion.29
  18.4 7.6 fusion.10
  26.0 0.0 copy-start.5
  26.0 0.4 copy.22
  26.4 23.2 %all_to_all.18 = bf16[4,128,512]{2,0,1:T(4,128)(2,1)S(1)} all-to-all(bf16[4,128,512]{2,0,1:T(4,128)(2,1)S(1)} %copy.22), channel_id=1, replica_groups=mesh['group'=2,'dev_0'=4,'dev_1'=2,'dev_2'=4,'dev_3'=2] {'dev_0','dev_1'..., dimensions={1} | all-to-all | bytes 1048576 | tf_op jit(solution)/shard_map/all_to_all | solution.py:56
  49.6 0.2 copy.27
  49.8 0.1 all_to_all.16
  49.9 0.0 copy-done.5
  49.9 0.3 convolution_convert_fusion.1
  50.3 0.0 copy-start.10
  50.3 0.0 copy-start.7
  50.3 0.0 copy-start.8
  50.3 0.0 copy-start.4
  50.3 0.0 copy-start.6
  50.3 5.0 convolution_convert_fusion
  55.3 0.0 all-reduce.5.cloned.1.call-update
  55.4 0.0 all-gather.3.cloned.1.call-start
  55.4 0.0 copy-done.10
  55.4 0.6 dynamic-slice
  56.7 0.0 copy-done.7
  56.7 0.0 copy-done.8
  56.7 0.1 select_reduce_fusion
  56.8 557.3 %all-reduce.5.cloned.1.call-done = bf16[256,7168]{1,0:T(8,128)(2,1)} async-done(((bf16[256,7168]{1,0:T(8,128)(2,1)}), bf16[256,7168]{1,0:T(8,128)(2,1)}) %all-reduce.5.cloned.1.call-update) | async-done | bytes 3670032
  614.1 0.0 copy-done.4
  614.1 1.1 multiply_reduce_fusion
  615.2 0.0 copy-done.6
  615.2 1.0 fusion.26
  616.2 0.7 maximum_bitcast_fusion
  616.9 0.0 all-gather.3.cloned.1.call-update
  616.9 0.2 all-reduce.7.cloned.1.call-start
  617.2 210.2 %all-gather.3.cloned.1.call-done = f32[128,4,7200]{2,1,0:T(4,128)} async-done(((f32[1,4,7200]{2,1,0:T(4,128)}), f32[128,4,7200]{2,1,0:T(4,128)}) %all-gather.3.cloned.1.call-update) | async-done | bytes 14745616 | tf_op jit(solution)/shard_map/all_gather | solution.py:74
  827.3 17.5 %reshape.25 = f32[512,7200]{1,0:T(8,128)} reshape(f32[128,4,7200]{2,1,0:T(4,128)} %all-gather.3.cloned.1.call-done) | data formatting | bytes 29491200
  844.8 1.1 fusion.21
  845.9 8.3 fusion.3
  854.2 0.0 copy-start.1
  854.2 18.2 %multiply_convert_fusion = bf16[512,7168]{1,0:T(8,128)(2,1)} fusion(f32[512]{0:T(512)S(1)} %fusion.21, bf16[1,256,7168]{2,1,0:T(8,128)(2,1)} %param.27, bf16[1,7168,256]{2,1,0:T(8,128)(2,1)} %param.26, f32[512,7200]{1,0:T(8,128)} %reshape.25, f32[512,256]{1,0:T(8,128)S(1)} %fusion.3), kind=kOutput, calls=%fused_computation.1 | convolution fusion | flops 3766222848 | bytes 22546432 | tf_op jit(solution)/shard_map/dot_general | solution.py:34
  872.4 0.0 all-reduce.7.cloned.1.call-update
  872.4 158.7 %all-reduce.7.cloned.1.call-done = bf16[512,7168]{1,0:T(8,128)(2,1)} async-done(((bf16[512,7168]{1,0:T(8,128)(2,1)}), bf16[512,7168]{1,0:T(8,128)(2,1)}) %all-reduce.7.cloned.1.call-update) | async-done | bytes 7340048
  1031.1 1.7 add_convert_fusion
  1032.7 0.0 copy-done.1
  (2 shorter events, 0.0 us)
Async XLA Ops:
  6.5 1.2 copy-start
  6.5 2.8 copy-start.3
  6.5 2.8 copy-start.9
  6.5 607.6 %all-reduce.5.cloned.1.call-start = ((), (), s32[]{:S(2)}) async-start(), calls=%async_computation.2 | async-start | bytes 7340032
  15.7 1.9 copy-start.2
  26.0 23.9 %copy-start.5 = (bf16[2,512,128]{2,1,0:T(8,128)(2,1)S(1)}, bf16[2,512,128]{2,1,0:T(8,128)(2,1)}, u32[]{:S(2)}) copy-start(bf16[2,512,128]{2,1,0:T(8,128)(2,1)} %param.19) | copy-start | bytes 786436
  50.3 5.2 copy-start.10
  50.3 6.4 copy-start.7
  50.3 6.4 copy-start.8
  50.3 563.8 %copy-start.4 = (bf16[4,7168]{1,0:T(4,128)(2,1)S(1)}, bf16[4,7168]{1,0:T(4,128)(2,1)}, u32[]{:S(2)}) copy-start(bf16[4,7168]{1,0:T(4,128)(2,1)} %param.21) | copy-start | bytes 172036
  50.3 564.9 %copy-start.6 = (f32[7168]{0:T(1024)S(1)}, f32[7168]{0:T(1024)}, u32[]{:S(2)}) copy-start(f32[7168]{0:T(1024)} %param.22) | copy-start | bytes 86020
  55.4 772.0 %all-gather.3.cloned.1.call-start = ((), (), s32[]{:S(2)}) async-start(), calls=%async_computation.1 | async-start | bytes 15058944 | tf_op jit(solution)/shard_map/all_gather | solution.py:74
  616.9 414.2 %all-reduce.7.cloned.1.call-start = ((), (), s32[]{:S(2)}) async-start(), calls=%async_computation.3 | async-start | bytes 14680064
  854.2 178.5 %copy-start.1 = (bf16[4,64,2048]{2,1,0:T(8,128)(2,1)S(1)}, bf16[4,64,2048]{2,1,0:T(8,128)(2,1)}, u32[]{:S(2)}) copy-start(bf16[4,64,2048]{2,1,0:T(8,128)(2,1)} %param.17) | copy-start | bytes 3145732
Sparse Core Ops, SparseCore 0:
  55.5 558.5 all-reduce.4
  617.0 210.2 all-gather.2
  872.5 158.4 all-reduce.6
